TPU v7x, 32 devices: a whole 2x2x4 slice. The times are simulated.
32 devices in a mesh: wide: 8 (over y, x, core), narrow: 4 (over z).
Axes of the slice: x: 2, y: 2, z: 4, core: 2. Of those that a mesh axis runs over, the one named last changes fastest.
Arguments:
- tokens: bfloat16 [10240, 2048], P(('wide', 'narrow')), may hold values from -6 to 6
- cotangent: bfloat16 [10240, 2048], P(('wide', 'narrow')), may hold values from -6 to 6
- lengths: int32 [32], P(('wide', 'narrow')), may hold values from 40 to 320, as said below
- positions: int32 [10240], P(('wide', 'narrow')), may hold values from 0 to 319, as said below
- norm_attn: bfloat16 [2048], P(('wide', 'narrow')), may hold values from 0.25 to 1.75
- w_query: bfloat16 [2048, 2048], P(('wide', 'narrow')), may hold values from -0.1875 to 0.1875
- w_key: bfloat16 [2048, 256], P(('wide', 'narrow')), may hold values from -0.1875 to 0.1875
- w_value: bfloat16 [2048, 256], P(('wide', 'narrow')), may hold values from -0.125 to 0.125
- w_output: bfloat16 [2048, 2048], P(('wide', 'narrow')), may hold values from -0.5 to 0.5
- norm_mlp: bfloat16 [2048], P(('wide', 'narrow')), may hold values from 0.25 to 1.75
- w_gate: bfloat16 [2048, 5632], P(('wide', 'narrow')), may hold values from -0.125 to 0.125
- w_up: bfloat16 [2048, 5632], P(('wide', 'narrow')), may hold values from -0.125 to 0.125
- w_down: bfloat16 [2048, 5632], P(('wide', 'narrow')), may hold values from -0.109375 to 0.109375
Outputs:
- output: bfloat16 [10240, 2048], P(('wide', 'narrow'))
- grad_tokens: float32 [10240, 2048], P(('wide', 'narrow'))
- grad_norm_attn: float32 [2048], P(('wide', 'narrow'))
- grad_w_query: float32 [2048, 2048], P(('wide', 'narrow'))
- grad_w_key: float32 [2048, 256], P(('wide', 'narrow'))
- grad_w_value: float32 [2048, 256], P(('wide', 'narrow'))
- grad_w_output: float32 [2048, 2048], P(('wide', 'narrow'))
- grad_norm_mlp: float32 [2048], P(('wide', 'narrow'))
- grad_w_gate: float32 [2048, 5632], P(('wide', 'narrow'))
- grad_w_up: float32 [2048, 5632], P(('wide', 'narrow'))
- grad_w_down: float32 [2048, 5632], P(('wide', 'narrow'))
Inputs may be any that keep to these rules, and one draw needn't show every extreme that they name: `lengths`: one sequence of every draw uses all 320 slots. Within a sequence positions rise by one from slot to slot and restart at 0 where a packed document starts; every sequence starts at position 0, and the first sequence holds a single document.
All inputs are finite; a program needn't handle non-finite values.
Results may differ from a plain program's by a relative error of at most 0.014.
The roundings to bfloat16 on the way count: a program that leaves them out, or rounds other values in their place, can miss the bound.
Values may be sent and summed in bfloat16 or wider, within the bound.
A program may use at most 384 MiB of HBM per device.

v0:
```python
import math
import jax
import jax.numpy as jnp
from jax import lax
from jax.sharding import PartitionSpec as P

QUERY_HEADS = 32
KEY_VALUE_HEADS = 4
HEAD_SIZE = 64
norm_eps = 1e-05
rope_base = 10000.0
masked_score = -1e30
contract_last = (((1,), (1,)), ((), ()))
contract_first = (((0,), (0,)), ((), ()))


def rope_tables(positions):
    half_dim = HEAD_SIZE // 2
    inv_freq = jnp.exp(
        -math.log(rope_base) * jnp.arange(half_dim, dtype=jnp.float32) * 2.0 / HEAD_SIZE
    )
    angles = positions.astype(jnp.float32)[..., None] * inv_freq
    cosine = jnp.cos(angles)
    sine_part = jnp.sin(angles)
    return (jnp.concatenate([cosine, cosine], -1), jnp.concatenate([sine_part, sine_part], -1))


def apply_rotary(values, cosine_table, sine_table):
    half_dim = values.shape[-1] // 2
    turned = jnp.concatenate([-values[..., half_dim:], values[..., :half_dim]], -1)
    return values * cosine_table[..., None, :] + turned * sine_table[..., None, :]


def invert_rotary(grad_rows, cosine_table, sine_table):
    half_dim = grad_rows.shape[-1] // 2
    with_cos = grad_rows * cosine_table[..., None, :]
    with_sin = grad_rows * sine_table[..., None, :]
    return with_cos + jnp.concatenate([with_sin[..., half_dim:], -with_sin[..., :half_dim]], -1)


def normalize(values):
    return values * lax.rsqrt(jnp.mean(values * values, axis=-1, keepdims=True) + norm_eps)


def norm_back(grad_hat, normed, values):
    row_scale = lax.rsqrt(jnp.mean(values * values, axis=-1, keepdims=True) + norm_eps)
    return row_scale * (grad_hat - normed * jnp.mean(grad_hat * normed, axis=-1, keepdims=True))


def attention_inputs(normed, norm_attn, w_query, w_key, w_value):
    gain_piece = lax.all_gather(norm_attn, ("wide", "narrow"), axis=0, tiled=True)
    query_rows = lax.all_gather(w_query, ("wide", "narrow"), axis=0, tiled=True)
    key_rows = lax.all_gather(w_key, ("wide", "narrow"), axis=0, tiled=True)
    value_rows = lax.all_gather(w_value, ("wide", "narrow"), axis=0, tiled=True)
    gain_float = gain_piece.astype(jnp.float32)
    columns = (normed * gain_float).astype(jnp.bfloat16)
    query_sum = jnp.dot(columns, query_rows, preferred_element_type=jnp.float32)
    key_sum = jnp.dot(columns, key_rows, preferred_element_type=jnp.float32)
    value_sum = jnp.dot(columns, value_rows, preferred_element_type=jnp.float32)
    return (gain_float, columns, query_sum, key_sum, value_sum)


def mlp_inputs(normed, norm_mlp, w_gate, w_up):
    gain_piece = lax.all_gather(norm_mlp, ("wide", "narrow"), axis=0, tiled=True)
    gate_rows = lax.all_gather(w_gate, ("wide", "narrow"), axis=0, tiled=True)
    up_rows = lax.all_gather(w_up, ("wide", "narrow"), axis=0, tiled=True)
    gain_float = gain_piece.astype(jnp.float32)
    columns = (normed * gain_float).astype(jnp.bfloat16)
    gate_sum = jnp.dot(columns, gate_rows, preferred_element_type=jnp.float32)
    up_sum = jnp.dot(columns, up_rows, preferred_element_type=jnp.float32)
    return (gain_float, columns, gate_sum, up_sum)


def head_slices(query_rotated, key_rotated, value_reduced, shared_key_head):
    row_total_count = query_rotated.shape[0]
    heads_per_group = QUERY_HEADS // KEY_VALUE_HEADS
    query_head = query_rotated[
        :,
        shared_key_head
        * heads_per_group
        * HEAD_SIZE : (shared_key_head + 1)
        * heads_per_group
        * HEAD_SIZE,
    ].reshape(row_total_count, heads_per_group, HEAD_SIZE)
    key_head = key_rotated[:, shared_key_head * HEAD_SIZE : (shared_key_head + 1) * HEAD_SIZE]
    value_head = value_reduced[:, shared_key_head * HEAD_SIZE : (shared_key_head + 1) * HEAD_SIZE]
    return (query_head, key_head, value_head)


def head_scores(query_head, key_head):
    row_total_count = query_head.shape[0]
    causal = jnp.arange(row_total_count)[:, None] >= jnp.arange(row_total_count)[None, :]
    raw_scores = jnp.einsum("qrd,kd->rqk", query_head, key_head, preferred_element_type=jnp.float32)
    return jnp.where(causal, raw_scores * HEAD_SIZE ** (-0.5), masked_score)


def attend(query_rotated, key_rotated, value_reduced):
    row_total_count = query_rotated.shape[0]
    heads_per_group = QUERY_HEADS // KEY_VALUE_HEADS
    contexts = []
    log_totals = []
    for shared_key_head in range(KEY_VALUE_HEADS):
        query_head, key_head, value_head = head_slices(
            query_rotated, key_rotated, value_reduced, shared_key_head
        )
        scores = head_scores(query_head, key_head)
        row_peak = jnp.max(scores, axis=-1, keepdims=True)
        exp_scores = jnp.exp(scores - row_peak)
        row_total = jnp.sum(exp_scores, axis=-1, keepdims=True)
        probs = exp_scores / row_total
        context_head = jnp.einsum(
            "rqk,kd->qrd",
            probs.astype(jnp.bfloat16),
            value_head,
            preferred_element_type=jnp.float32,
        )
        contexts.append(context_head.reshape(row_total_count, heads_per_group * HEAD_SIZE))
        log_totals.append(row_peak + jnp.log(row_total))
    return (jnp.concatenate(contexts, 1).astype(jnp.bfloat16), log_totals)


def attend_back(query_rotated, key_rotated, value_reduced, log_totals, grad_context):
    row_total_count = query_rotated.shape[0]
    heads_per_group = QUERY_HEADS // KEY_VALUE_HEADS
    score_scale = HEAD_SIZE ** (-0.5)
    query_grads = []
    key_grads = []
    value_grads = []
    for shared_key_head in range(KEY_VALUE_HEADS):
        query_head, key_head, value_head = head_slices(
            query_rotated, key_rotated, value_reduced, shared_key_head
        )
        scores = head_scores(query_head, key_head)
        probs = jnp.exp(scores - log_totals[shared_key_head])
        probs_low = probs.astype(jnp.bfloat16)
        grad_head = grad_context[
            :,
            shared_key_head
            * heads_per_group
            * HEAD_SIZE : (shared_key_head + 1)
            * heads_per_group
            * HEAD_SIZE,
        ].reshape(row_total_count, heads_per_group, HEAD_SIZE)
        grad_probs = jnp.einsum(
            "qrd,kd->rqk", grad_head, value_head, preferred_element_type=jnp.float32
        )
        value_grads.append(
            jnp.einsum("rqk,qrd->kd", probs_low, grad_head, preferred_element_type=jnp.float32)
        )
        inner_sum = jnp.sum(grad_probs * probs, axis=-1, keepdims=True)
        grad_scores = (probs * (grad_probs - inner_sum) * score_scale).astype(jnp.bfloat16)
        query_grad = jnp.einsum(
            "rqk,kd->qrd", grad_scores, key_head, preferred_element_type=jnp.float32
        )
        query_grads.append(query_grad.reshape(row_total_count, heads_per_group * HEAD_SIZE))
        key_grads.append(
            jnp.einsum("rqk,qrd->kd", grad_scores, query_head, preferred_element_type=jnp.float32)
        )
    return (
        jnp.concatenate(query_grads, 1),
        jnp.concatenate(key_grads, 1),
        jnp.concatenate(value_grads, 1),
    )


def make_term(width_sides, other_sides):
    down_side, mlp_side, attn_side, qkv_side = width_sides
    mixed_rows, gate_rows, up_rows, context_rows, query_rows, key_rows, value_rows = other_sides

    def grad_term(first_row, row_span):
        pieces = [
            lax.dot_general(
                down_side, mixed_rows, contract_first, preferred_element_type=jnp.float32
            ),
            lax.dot_general(
                mlp_side, gate_rows, contract_first, preferred_element_type=jnp.float32
            ),
            lax.dot_general(mlp_side, up_rows, contract_first, preferred_element_type=jnp.float32),
            lax.dot_general(
                attn_side, context_rows, contract_first, preferred_element_type=jnp.float32
            ),
            lax.dot_general(
                qkv_side, query_rows, contract_first, preferred_element_type=jnp.float32
            ),
            lax.dot_general(qkv_side, key_rows, contract_first, preferred_element_type=jnp.float32),
            lax.dot_general(
                qkv_side, value_rows, contract_first, preferred_element_type=jnp.float32
            ),
        ]
        return jnp.concatenate(pieces, 1)

    return grad_term


def per_device(
    tokens,
    cotangent,
    lengths,
    positions,
    norm_attn,
    w_query,
    w_key,
    w_value,
    w_output,
    norm_mlp,
    w_gate,
    w_up,
    w_down,
):
    row_total_count = tokens.shape[0]
    shard_rows = w_query.shape[0]
    query_width = w_query.shape[1]
    key_width = w_key.shape[1]
    hidden_width = w_gate.shape[1]
    inputs = tokens.astype(jnp.float32)
    valid_rows = (jnp.arange(row_total_count) < lengths[0]).astype(jnp.float32)[:, None]
    cosine_table, sine_table = rope_tables(positions)
    normed_attn = normalize(inputs)
    gain_attn_full, scaled_attn, query_pre, key_unrotated, value_pre = attention_inputs(
        normed_attn, norm_attn, w_query, w_key, w_value
    )
    query_rotated = (
        apply_rotary(
            query_pre.reshape(row_total_count, QUERY_HEADS, HEAD_SIZE), cosine_table, sine_table
        )
        .reshape(row_total_count, query_width)
        .astype(jnp.bfloat16)
    )
    key_rotated = (
        apply_rotary(
            key_unrotated.reshape(row_total_count, KEY_VALUE_HEADS, HEAD_SIZE),
            cosine_table,
            sine_table,
        )
        .reshape(row_total_count, key_width)
        .astype(jnp.bfloat16)
    )
    value_reduced = value_pre.astype(jnp.bfloat16)
    context, log_totals = attend(query_rotated, key_rotated, value_reduced)
    attn_out = lax.dot_general(
        context,
        lax.all_gather(w_output, ("wide", "narrow"), axis=0, tiled=True),
        contract_last,
        preferred_element_type=jnp.float32,
    )
    hidden = inputs + attn_out
    normed_mlp = normalize(hidden)
    gain_mlp_full, scaled_mlp, gate_proj, up_proj = mlp_inputs(normed_mlp, norm_mlp, w_gate, w_up)
    mixed_low = (gate_proj * jax.nn.sigmoid(gate_proj) * up_proj).astype(jnp.bfloat16)
    mlp_out = lax.dot_general(
        mixed_low,
        lax.all_gather(w_down, ("wide", "narrow"), axis=0, tiled=True),
        contract_last,
        preferred_element_type=jnp.float32,
    )
    output = (valid_rows * (hidden + mlp_out)).astype(jnp.bfloat16)
    grad_y = cotangent.astype(jnp.float32) * valid_rows
    grad_y_low = grad_y.astype(jnp.bfloat16)
    grad_cols = grad_y_low
    grad_mixed = jnp.dot(
        grad_cols,
        lax.all_gather(w_down, ("wide", "narrow"), axis=0, tiled=True),
        preferred_element_type=jnp.float32,
    )
    again_values = mlp_inputs(normed_mlp, norm_mlp, w_gate, w_up)
    gate_proj = again_values[2]
    up_proj = again_values[3]
    sigmoid_gate = jax.nn.sigmoid(gate_proj)
    grad_gate = (
        grad_mixed * up_proj * (sigmoid_gate * (1.0 + gate_proj * (1.0 - sigmoid_gate)))
    ).astype(jnp.bfloat16)
    grad_up = (grad_mixed * (gate_proj * sigmoid_gate)).astype(jnp.bfloat16)
    gate_rows = lax.all_gather(w_gate, ("wide", "narrow"), axis=0, tiled=True)
    up_rows = lax.all_gather(w_up, ("wide", "narrow"), axis=0, tiled=True)
    columns = lax.dot_general(
        grad_gate, gate_rows, contract_last, preferred_element_type=jnp.float32
    )
    columns = columns + lax.dot_general(
        grad_up, up_rows, contract_last, preferred_element_type=jnp.float32
    )
    grad_xn2 = columns
    grad_gain_mlp = jnp.sum(grad_xn2 * normed_mlp, axis=0)
    grad_hidden = grad_y + norm_back(grad_xn2 * gain_mlp_full, normed_mlp, hidden)
    grad_attn_low = grad_hidden.astype(jnp.bfloat16)
    grad_cols = grad_attn_low
    grad_context = jnp.dot(
        grad_cols,
        lax.all_gather(w_output, ("wide", "narrow"), axis=0, tiled=True),
        preferred_element_type=jnp.float32,
    )
    grad_context = grad_context.astype(jnp.bfloat16)
    grad_query_rot, gradient_key_rotated, grad_value_sum = attend_back(
        query_rotated, key_rotated, value_reduced, log_totals, grad_context
    )
    grad_query = (
        invert_rotary(
            grad_query_rot.reshape(row_total_count, QUERY_HEADS, HEAD_SIZE),
            cosine_table,
            sine_table,
        )
        .reshape(row_total_count, query_width)
        .astype(jnp.bfloat16)
    )
    grad_key = (
        invert_rotary(
            gradient_key_rotated.reshape(row_total_count, KEY_VALUE_HEADS, HEAD_SIZE),
            cosine_table,
            sine_table,
        )
        .reshape(row_total_count, key_width)
        .astype(jnp.bfloat16)
    )
    grad_value = grad_value_sum.astype(jnp.bfloat16)
    query_rows = lax.all_gather(w_query, ("wide", "narrow"), axis=0, tiled=True)
    key_rows = lax.all_gather(w_key, ("wide", "narrow"), axis=0, tiled=True)
    value_rows = lax.all_gather(w_value, ("wide", "narrow"), axis=0, tiled=True)
    columns = lax.dot_general(
        grad_query, query_rows, contract_last, preferred_element_type=jnp.float32
    )
    columns = columns + lax.dot_general(
        grad_key, key_rows, contract_last, preferred_element_type=jnp.float32
    )
    columns = columns + lax.dot_general(
        grad_value, value_rows, contract_last, preferred_element_type=jnp.float32
    )
    local_term = make_term(
        (grad_y_low, scaled_mlp, grad_attn_low, scaled_attn),
        (mixed_low, grad_gate, grad_up, context, grad_query, grad_key, grad_value),
    )
    all_sums = lax.psum_scatter(
        local_term(jnp.int32(0), lax.axis_size(("wide", "narrow")) * shard_rows),
        ("wide", "narrow"),
        scatter_dimension=0,
        tiled=True,
    )
    edges = [0]
    for width in (
        hidden_width,
        hidden_width,
        hidden_width,
        query_width,
        query_width,
        key_width,
        key_width,
    ):
        edges.append(edges[-1] + width)
    grad_w_down = all_sums[:, edges[0] : edges[1]]
    grad_w_gate = all_sums[:, edges[1] : edges[2]]
    grad_w_up = all_sums[:, edges[2] : edges[3]]
    grad_w_output = all_sums[:, edges[3] : edges[4]]
    grad_w_query = all_sums[:, edges[4] : edges[5]]
    grad_w_key = all_sums[:, edges[5] : edges[6]]
    grad_w_value = all_sums[:, edges[6] : edges[7]]
    grad_gain_attn = jnp.sum(columns * normed_attn, axis=0)
    grad_tokens = grad_hidden + norm_back(columns * gain_attn_full, normed_attn, inputs)
    grad_norm_attn, grad_norm_mlp = (
        lax.psum_scatter(grad_gain_attn, ("wide", "narrow"), scatter_dimension=0, tiled=True),
        lax.psum_scatter(grad_gain_mlp, ("wide", "narrow"), scatter_dimension=0, tiled=True),
    )
    return (
        output,
        grad_tokens,
        grad_norm_attn,
        grad_w_query,
        grad_w_key,
        grad_w_value,
        grad_w_output,
        grad_norm_mlp,
        grad_w_gate,
        grad_w_up,
        grad_w_down,
    )


def solution(mesh):
    in_specs = (
        P(("wide", "narrow"), None),
        P(("wide", "narrow"), None),
        P(("wide", "narrow")),
        P(("wide", "narrow")),
        P(("wide", "narrow")),
        P(("wide", "narrow"), None),
        P(("wide", "narrow"), None),
        P(("wide", "narrow"), None),
        P(("wide", "narrow"), None),
        P(("wide", "narrow")),
        P(("wide", "narrow"), None),
        P(("wide", "narrow"), None),
        P(("wide", "narrow"), None),
    )
    out_specs = (
        P(("wide", "narrow"), None),
        P(("wide", "narrow"), None),
        P(("wide", "narrow")),
        P(("wide", "narrow"), None),
        P(("wide", "narrow"), None),
        P(("wide", "narrow"), None),
        P(("wide", "narrow"), None),
        P(("wide", "narrow")),
        P(("wide", "narrow"), None),
        P(("wide", "narrow"), None),
        P(("wide", "narrow"), None),
    )
    return jax.shard_map(
        per_device, mesh=mesh, in_specs=in_specs, out_specs=out_specs, check_vma=False
    )
```

profile of v0, /device:TPU:0, one launch (start us, length us, event | category | flops | bytes accessed | tf_op | source)
XLA Modules:
  0.0 2423.2 jit_solution(7380186025434072481)
XLA Ops:
  15.0 42.1 %all-reduce.5 = (bf16[2048]{0:T(1024)(128)(2,1)S(1)}, bf16[2048]{0:T(1024)(128)(2,1)S(1)}) all-reduce(bf16[2048]{0:T(1024)(128)(2,1)S(1)} %dynamic-update-slice, bf16[2048]{0:T(1024)(128)(2,1)S(1)} %dynamic-update-slice.1), channel_id=1, replica_groups=mesh['wide'=8,'narrow'=4] {'wide','narrow'}, use_global_device_ids=true, to_apply=%add | all-reduce | flops 4096 | bytes 16384
  57.6 2.0 mul.301
  59.6 3.4 copy.141
  63.4 4.1 all-gather.10.cloned.1.call-done
  67.5 1.8 fusion.146
  69.8 53.6 %all-gather.8.cloned.1.call-done = bf16[2048,256]{1,0:T(8,128)(2,1)} async-done(((bf16[64,256]{1,0:T(8,128)(2,1)}), bf16[2048,256]{1,0:T(8,128)(2,1)}) %all-gather.8.cloned.1.call-update) | async-done | bytes 1048592 | tf_op jit(solution)/shard_map/all_gather | solution.py:54
  123.4 2.5 convolution_convert_fusion.1
  125.8 76.9 %all-gather.12.cloned.1.call-done = bf16[2048,2048]{1,0:T(8,128)(2,1)} async-done(((bf16[64,2048]{1,0:T(8,128)(2,1)}), bf16[2048,2048]{1,0:T(8,128)(2,1)}) %all-gather.12.cloned.1.call-update) | async-done | bytes 8388624 | tf_op jit(solution)/shard_map/all_gather | solution.py:52
  202.7 7.8 fusion.144
  210.5 3.5 copy.142
  214.0 2.1 slice_negate_fusion.1
  216.1 1.9 maximum_multiply_fusion
  218.1 3.6 copy.143
  221.6 3.9 add_convert_fusion
  227.1 1.3 copy.148
  236.7 1.6 fusion.81
  238.2 43.3 %all-gather.14.cloned.1.call-done = bf16[2048,2048]{1,0:T(8,128)(2,1)} async-done(((bf16[64,2048]{1,0:T(8,128)(2,1)}), bf16[2048,2048]{1,0:T(8,128)(2,1)}) %all-gather.14.cloned.1.call-update) | async-done | bytes 8388624 | tf_op jit(solution)/shard_map/all_gather | solution.py:242
  281.5 7.5 multiply_reduce_fusion.2
  291.4 136.0 %all-gather.18.cloned.1.call-done = bf16[2048,5632]{1,0:T(8,128)(2,1)} async-done(((bf16[64,5632]{1,0:T(8,128)(2,1)}), bf16[2048,5632]{1,0:T(8,128)(2,1)}) %all-gather.18.cloned.1.call-update) | async-done | bytes 23068688 | tf_op jit(solution)/shard_map/all_gather | solution.py:66
  427.4 14.9 fusion.161
  442.3 130.6 %all-gather.16.cloned.1.call-done = bf16[2048,5632]{1,0:T(8,128)(2,1)} async-done(((bf16[64,5632]{1,0:T(8,128)(2,1)}), bf16[2048,5632]{1,0:T(8,128)(2,1)}) %all-gather.16.cloned.1.call-update) | async-done | bytes 23068688 | tf_op jit(solution)/shard_map/all_gather | solution.py:65
  572.9 14.9 fusion.160
  587.8 130.7 %all-gather.20.cloned.1.call-done = bf16[2048,5632]{1,0:T(8,128)(2,1)} async-done(((bf16[64,5632]{1,0:T(8,128)(2,1)}), bf16[2048,5632]{1,0:T(8,128)(2,1)}) %all-gather.20.cloned.1.call-update) | async-done | bytes 23068688 | tf_op jit(solution)/shard_map/all_gather | solution.py:252
  718.6 20.5 multiply_convert_fusion
  739.0 14.3 fusion.162
  753.4 15.6 multiply_reduce_fusion
  769.0 3.7 multiply_add_fusion
  772.8 6.2 convolution_convert_fusion
  779.0 1.1 fusion.153
  780.1 1.2 copy.164
  781.3 3.6 fusion.117
  785.7 7.3 fusion.83
  793.0 8.2 fusion.75
  801.5 3.5 fusion.118
  805.0 2.1 fusion.101
  807.1 8.2 fusion.84
  815.3 8.7 fusion.76
  824.3 3.6 fusion.119
  827.9 2.1 fusion.98
  830.0 8.0 fusion.85
  838.0 8.3 fusion.77
  846.6 3.6 fusion.116
  850.2 2.1 fusion.107
  852.3 8.0 fusion.82
  860.3 8.2 fusion.74
  870.4 2.5 pad_maximum_fusion
  872.9 2.0 fusion.152
  874.9 23.4 convolution_dynamic-update-slice_fusion.2
  898.3 23.2 convolution_dynamic-update-slice_fusion.1
  921.4 20.5 convolution_dynamic-update-slice_fusion
  942.0 9.8 convolution_dynamic-update-slice_fusion.4
  952.1 1.6 copy-done.13
  955.1 8.6 convolution_dynamic-update-slice_fusion.3
  963.7 2.3 convolution_dynamic-update-slice_fusion.6
  966.0 2.3 convolution_dynamic-update-slice_fusion.5
  968.3 7.0 fusion.163
  977.4 2.7 fusion.37
  980.2 38.6 %all-reduce.4 = (f32[2048]{0:T(1024)S(1)}, f32[2048]{0:T(1024)S(1)}) all-reduce(f32[2048]{0:T(1024)S(1)} %get-tuple-element.13, f32[2048]{0:T(1024)S(1)} %copy-done.66), channel_id=2, replica_groups=mesh['wide'=8,'narrow'=4] {'wide','narrow'}, use_global_device_ids=true, to_apply=%region_17.18.clone | all-reduce | flops 4096 | bytes 32768
  1020.0 5.0 fusion.36
  1025.0 19.3 fusion.31
  1044.3 1363.6 %reduce-scatter.2.cloned.1.call-done = f32[64,21504]{1,0:T(8,128)} async-done(((f32[2048,21504]{1,0:T(8,128)}), f32[64,21504]{1,0:T(8,128)}) %reduce-scatter.2.cloned.1.call-update) | async-done | bytes 5505040 | tf_op jit(solution)/shard_map/reduce_scatter | solution.py:330
  2407.9 1.5 fusion.151
  2409.4 2.3 fusion.150
  2411.7 4.4 fusion.149
  (208 shorter events, 28.4 us)
Async XLA Ops:
  7.2 60.4 %all-gather.10.cloned.1.call-start = ((), (), s32[]{:S(2)}) async-start(), calls=%async_computation.2 | async-start | bytes 1081344 | tf_op jit(solution)/shard_map/all_gather | solution.py:53
  7.9 115.4 %all-gather.8.cloned.1.call-start = ((), (), s32[]{:S(2)}) async-start(), calls=%async_computation.1 | async-start | bytes 1081344 | tf_op jit(solution)/shard_map/all_gather | solution.py:54
  8.7 194.0 %all-gather.12.cloned.1.call-start = ((), (), s32[]{:S(2)}) async-start(), calls=%async_computation.3 | async-start | bytes 8650752 | tf_op jit(solution)/shard_map/all_gather | solution.py:52
  9.4 272.1 %all-gather.14.cloned.1.call-start = ((), (), s32[]{:S(2)}) async-start(), calls=%async_computation.4 | async-start | bytes 8650752 | tf_op jit(solution)/shard_map/all_gather | solution.py:242
  10.0 417.4 %all-gather.18.cloned.1.call-start = ((), (), s32[]{:S(2)}) async-start(), calls=%async_computation.6 | async-start | bytes 23789568 | tf_op jit(solution)/shard_map/all_gather | solution.py:66
  10.6 562.3 %all-gather.16.cloned.1.call-start = ((), (), s32[]{:S(2)}) async-start(), calls=%async_computation.5 | async-start | bytes 23789568 | tf_op jit(solution)/shard_map/all_gather | solution.py:65
  11.1 707.4 %all-gather.20.cloned.1.call-start = ((), (), s32[]{:S(2)}) async-start(), calls=%async_computation.7 | async-start | bytes 23789568 | tf_op jit(solution)/shard_map/all_gather | solution.py:252
  11.9 2396.0 %reduce-scatter.2.cloned.1.call-start = ((), (), s32[]{:S(2)}) async-start(), calls=%async_computation.8 | async-start | bytes 181665792 | tf_op jit(solution)/shard_map/reduce_scatter | solution.py:330
  57.1 145.6 %copy-start.55 = (f32[2048]{0:T(1024)}, f32[2048]{0:T(1024)S(1)}, u32[]{:S(2)}) copy-start(f32[2048]{0:T(1024)S(1)} %convert_element_type.106) | copy-start | bytes 24580
  57.4 5.6 copy-start.20
  57.6 5.5 copy-start.8
  62.9 706.1 %copy-start.57 = (f32[320]{0:T(512)}, f32[320]{0:T(512)S(1)}, u32[]{:S(2)}) copy-start(f32[320]{0:T(512)S(1)} %fusion.120) | copy-start | bytes 3844
  63.0 153.2 %copy-start.22 = (f32[320,64]{0,1:T(8,128)}, f32[320,64]{0,1:T(8,128)S(1)}, u32[]{:S(2)}) copy-start(f32[320,64]{0,1:T(8,128)S(1)} %pad_maximum_fusion.9) | copy-start | bytes 245764
  63.4 139.3 %copy-start.59 = (f32[320]{0:T(512)}, f32[320]{0:T(512)S(1)}, u32[]{:S(2)}) copy-start(f32[320]{0:T(512)S(1)} %add_rsqrt_fusion.1) | copy-start | bytes 3844
  69.8 162.9 %copy-start.30 = (bf16[320,256]{1,0:T(8,128)(2,1)}, bf16[320,256]{1,0:T(8,128)(2,1)S(1)}, u32[]{:S(2)}) copy-start(bf16[320,256]{1,0:T(8,128)(2,1)S(1)} %add_convert_fusion.1) | copy-start | bytes 491524
  226.6 6.1 copy-start.24
  226.8 4.4 copy-start.26
  227.1 2.8 copy-start.28
  229.3 4.8 copy-start.6
  230.6 4.3 copy-start.4
  232.1 3.7 copy-start.2
  233.5 3.1 copy-start
  235.0 46.5 %copy-start.48 = (bf16[64,8,320]{2,0,1:T(8,128)(2,1)}, bf16[64,8,320]{2,0,1:T(8,128)(2,1)S(1)}, u32[]{:S(2)}) copy-start(bf16[64,8,320]{2,0,1:T(8,128)(2,1)S(1)} %fusion.80) | copy-start | bytes 983044
  235.8 45.7 %copy-start.50 = (bf16[64,8,320]{2,0,1:T(8,128)(2,1)}, bf16[64,8,320]{2,0,1:T(8,128)(2,1)S(1)}, u32[]{:S(2)}) copy-start(bf16[64,8,320]{2,0,1:T(8,128)(2,1)S(1)} %fusion.79) | copy-start | bytes 983044
  236.7 44.8 %copy-start.51 = (bf16[64,8,320]{2,0,1:T(8,128)(2,1)}, bf16[64,8,320]{2,0,1:T(8,128)(2,1)S(1)}, u32[]{:S(2)}) copy-start(bf16[64,8,320]{2,0,1:T(8,128)(2,1)S(1)} %fusion.78) | copy-start | bytes 983044
  289.0 2.1 copy-start.14
  289.1 495.8 %copy-start.64 = (f32[8,320]{1,0:T(8,128)}, f32[8,320]{1,0:T(8,128)S(1)}, u32[]{:S(2)}) copy-start(f32[8,320]{1,0:T(8,128)S(1)} %log_add_fusion.2) | copy-start | bytes 30724
  291.4 281.5 %copy-start.11 = (bf16[320,2048]{1,0:T(8,128)(2,1)}, bf16[320,2048]{1,0:T(8,128)(2,1)S(1)}, u32[]{:S(2)}) copy-start(bf16[320,2048]{1,0:T(8,128)(2,1)S(1)} %multiply_convert_fusion.3) | copy-start | bytes 3932164
  442.3 276.2 %copy-start.16 = (bf16[320,2048]{1,0:T(8,128)(2,1)S(1)}, bf16[320,2048]{1,0:T(8,128)(2,1)}, u32[]{:S(2)}) copy-start(bf16[320,2048]{1,0:T(8,128)(2,1)} %param.14) | copy-start | bytes 3932164
  739.0 14.3 copy-start.15
  781.3 3.6 copy-start.7
  785.7 7.3 copy-start.31
  785.7 7.3 copy-start.65
  793.0 8.2 copy-start.37
  801.5 3.6 copy-start.5
  801.5 5.7 copy-start.29
  807.1 8.2 copy-start.32
  807.1 8.2 copy-start.63
  815.3 8.7 copy-start.36
  824.2 3.6 copy-start.3
  824.2 5.7 copy-start.27
  830.0 8.0 copy-start.33
  830.0 8.1 copy-start.62
  838.0 8.4 copy-start.35
  846.6 3.6 copy-start.1
  846.6 5.7 copy-start.25
  852.3 8.0 copy-start.34
  852.3 8.0 copy-start.61
  860.2 8.3 copy-start.45
  860.2 8.3 copy-start.46
  860.2 8.3 copy-start.47
  860.2 8.4 copy-start.23
  860.3 8.5 copy-start.21
  898.3 23.2 copy-start.12
  921.4 20.5 copy-start.49
  942.0 9.8 copy-start.18
  942.0 9.8 copy-start.19
  955.0 8.6 copy-start.17
  955.0 10.9 copy-start.52
  955.0 10.9 copy-start.53
  955.0 10.9 copy-start.54
  968.3 7.0 copy-start.38
  975.3 2.1 copy-start.39
  977.4 2.7 copy-start.66
  (11 other events, 16.8 us)
Sparse Core Ops, SparseCore 0:
  11.0 56.4 all-gather.9
  70.5 52.8 all-gather.7
  126.3 76.3 all-gather.11
  205.5 75.9 all-gather.13
  284.2 143.1 all-gather.17
  430.1 142.7 all-gather.15
  575.7 142.7 all-gather.19
  968.4 1439.4 reduce-scatter.1
where the time goes:
time: 2430 us; the launch traced here: 2420 us
  waiting for transfers between devices  1940 us (80%)
  matrix products  319 us (13%)
  blocking collectives  80.7 us (3%)
  local copies, waits for them, and re-layouts  35.2 us (1%)
  other arithmetic  28.4 us (1%)
    reduce_scatter x1, waiting for transfers between devices, per_device(): lax.psum_scatter(local_term(jnp.int32(0), lax.axis_size(('wide', 'narrow'...  1360 us
    all_gather x1, waiting for transfers between devices, mlp_inputs(): up_rows = lax.all_gather(w_up, ('wide', 'narrow'), axis=0, tiled=True)  136 us
    all_gather x1, waiting for transfers between devices, per_device(): lax.all_gather(w_down, ('wide', 'narrow'), axis=0, tiled=True)  131 us
    all_gather x1, waiting for transfers between devices, mlp_inputs(): gate_rows = lax.all_gather(w_gate, ('wide', 'narrow'), axis=0, tiled=True)  131 us
    unnamed x2, blocking collectives  80.7 us
    all_gather x1, waiting for transfers between devices, attention_inputs(): query_rows = lax.all_gather(w_query, ('wide', 'narrow'), axis=0, tiled=True)  76.9 us
    all_gather x1, waiting for transfers between devices, attention_inputs(): value_rows = lax.all_gather(w_value, ('wide', 'narrow'), axis=0, tiled=True)  53.6 us
  transfers between devices with their start and end apart: 8, of which 8 were waited for; matrix products, arithmetic and copies ran while one was open for 5% of the time, Pallas kernels for 0%

commit v1 on v0

--- a/solution.py
+++ b/solution.py
@@ -50,8 +50,13 @@
 def attention_inputs(normed, norm_attn, w_query, w_key, w_value):
     gain_piece = lax.all_gather(norm_attn, ("wide", "narrow"), axis=0, tiled=True)
     query_rows = lax.all_gather(w_query, ("wide", "narrow"), axis=0, tiled=True)
-    key_rows = lax.all_gather(w_key, ("wide", "narrow"), axis=0, tiled=True)
-    value_rows = lax.all_gather(w_value, ("wide", "narrow"), axis=0, tiled=True)
+    key_rows, value_rows = jnp.split(
+        lax.all_gather(
+            jnp.concatenate([w_key, w_value], axis=1), ("wide", "narrow"), axis=0, tiled=True
+        ),
+        [w_key.shape[1]],
+        axis=1,
+    )
     gain_float = gain_piece.astype(jnp.float32)
     columns = (normed * gain_float).astype(jnp.bfloat16)
     query_sum = jnp.dot(columns, query_rows, preferred_element_type=jnp.float32)

time: 2430 us -> 2380 us (0.979)
  waiting for transfers between devices: 1940 us -> 1880 us
    all_gather x2 -> x3, waiting for transfers between devices: 57.7 us -> 6.96 us  [the longest x1 6.95 us: attention_inputs(): lax.all_gather(jnp.concatenate([w_key, w_value], axis=1), ('wide', 'narro...]
  transfers between devices with their start and end apart: 8 -> 9, of which waited for: 8 -> 7; matrix products, arithmetic and copies ran while one was open for 5% -> 16% of each run, Pallas kernels for 0% -> 0%
where the time goes in v1:
time: 2380 us; the launch traced here: 2370 us
  waiting for transfers between devices  1880 us (79%)
  matrix products  328 us (14%)
  blocking collectives  80.9 us (3%)
  local copies, waits for them, and re-layouts  38.7 us (2%)
  other arithmetic  31.4 us (1%)
    reduce_scatter x1, waiting for transfers between devices, per_device(): lax.psum_scatter(local_term(jnp.int32(0), lax.axis_size(('wide', 'narrow'...  1350 us
    all_gather x1, waiting for transfers between devices, mlp_inputs(): up_rows = lax.all_gather(w_up, ('wide', 'narrow'), axis=0, tiled=True)  137 us
    all_gather x1, waiting for transfers between devices, mlp_inputs(): gate_rows = lax.all_gather(w_gate, ('wide', 'narrow'), axis=0, tiled=True)  131 us
    all_gather x1, waiting for transfers between devices, per_device(): lax.all_gather(w_down, ('wide', 'narrow'), axis=0, tiled=True)  131 us
    unnamed x2, blocking collectives  80.9 us
    all_gather x1, waiting for transfers between devices, attention_inputs(): query_rows = lax.all_gather(w_query, ('wide', 'narrow'), axis=0, tiled=True)  74.4 us
  transfers between devices with their start and end apart: 9, of which 7 were waited for; matrix products, arithmetic and copies ran while one was open for 16% of the time, Pallas kernels for 0%

profile of v1, /device:TPU:0, one launch (start us, length us, event | category | flops | bytes accessed | tf_op | source)
XLA Modules:
  0.0 2374.3 jit_solution(12514624998021287632)
XLA Ops:
  7.3 1.5 pad_maximum_fusion.10
  15.9 42.1 %all-reduce.5 = (bf16[2048]{0:T(1024)(128)(2,1)S(1)}, bf16[2048]{0:T(1024)(128)(2,1)S(1)}) all-reduce(bf16[2048]{0:T(1024)(128)(2,1)S(1)} %dynamic-update-slice, bf16[2048]{0:T(1024)(128)(2,1)S(1)} %dynamic-update-slice.1), channel_id=1, replica_groups=mesh['wide'=8,'narrow'=4] {'wide','narrow'}, use_global_device_ids=true, to_apply=%add | all-reduce | flops 4096 | bytes 16384
  58.5 2.0 mul.301
  60.4 3.4 copy.141
  63.8 7.0 all-gather.9.cloned.1.call-done
  70.8 1.8 fusion.110
  73.0 2.5 convolution_convert_fusion.1
  75.6 74.4 %all-gather.11.cloned.1.call-done = bf16[2048,2048]{1,0:T(8,128)(2,1)} async-done(((bf16[64,2048]{1,0:T(8,128)(2,1)}), bf16[2048,2048]{1,0:T(8,128)(2,1)}) %all-gather.11.cloned.1.call-update) | async-done | bytes 8388624 | tf_op jit(solution)/shard_map/all_gather | solution.py:52
  150.0 7.8 fusion.147
  157.8 3.5 copy.142
  161.2 2.1 slice_negate_fusion.1
  163.4 1.9 maximum_multiply_fusion
  165.3 3.9 copy.143
  169.3 3.9 add_convert_fusion
  175.2 1.6 fusion.80
  178.2 1.6 fusion.79
  181.5 1.6 fusion.78
  186.1 1.6 fusion.81
  187.7 41.3 %all-gather.13.cloned.1.call-done = bf16[2048,2048]{1,0:T(8,128)(2,1)} async-done(((bf16[64,2048]{1,0:T(8,128)(2,1)}), bf16[2048,2048]{1,0:T(8,128)(2,1)}) %all-gather.13.cloned.1.call-update) | async-done | bytes 8388624 | tf_op jit(solution)/shard_map/all_gather | solution.py:247
  228.9 7.3 multiply_reduce_fusion.2
  238.0 136.8 %all-gather.17.cloned.1.call-done = bf16[2048,5632]{1,0:T(8,128)(2,1)} async-done(((bf16[64,5632]{1,0:T(8,128)(2,1)}), bf16[2048,5632]{1,0:T(8,128)(2,1)}) %all-gather.17.cloned.1.call-update) | async-done | bytes 23068688 | tf_op jit(solution)/shard_map/all_gather | solution.py:71
  374.9 14.9 fusion.163
  389.8 130.6 %all-gather.15.cloned.1.call-done = bf16[2048,5632]{1,0:T(8,128)(2,1)} async-done(((bf16[64,5632]{1,0:T(8,128)(2,1)}), bf16[2048,5632]{1,0:T(8,128)(2,1)}) %all-gather.15.cloned.1.call-update) | async-done | bytes 23068688 | tf_op jit(solution)/shard_map/all_gather | solution.py:70
  520.4 14.9 fusion.162
  535.3 130.6 %all-gather.19.cloned.1.call-done = bf16[2048,5632]{1,0:T(8,128)(2,1)} async-done(((bf16[64,5632]{1,0:T(8,128)(2,1)}), bf16[2048,5632]{1,0:T(8,128)(2,1)}) %all-gather.19.cloned.1.call-update) | async-done | bytes 23068688 | tf_op jit(solution)/shard_map/all_gather | solution.py:257
  665.9 20.4 multiply_convert_fusion
  686.3 14.3 fusion.164
  700.6 15.8 multiply_reduce_fusion
  716.5 3.8 multiply_add_fusion
  720.2 6.2 convolution_convert_fusion
  728.8 3.5 fusion.120
  732.2 8.0 fusion.83
  740.2 8.3 fusion.75
  749.7 3.4 fusion.121
  753.1 8.3 fusion.84
  761.4 8.4 fusion.76
  769.8 1.9 copy.172
  771.7 3.6 fusion.122
  775.3 8.1 fusion.85
  783.4 8.2 fusion.77
  791.6 1.9 copy.160
  793.5 3.6 fusion.119
  797.1 8.1 fusion.82
  805.2 8.3 fusion.74
  815.4 4.3 pad_maximum_fusion
  819.6 2.0 fusion.154
  821.6 23.2 convolution_dynamic-update-slice_fusion.2
  844.8 23.0 convolution_dynamic-update-slice_fusion.1
  867.8 20.7 convolution_dynamic-update-slice_fusion
  888.6 10.0 convolution_dynamic-update-slice_fusion.4
  898.8 1.6 copy-done.12
  901.8 8.6 convolution_dynamic-update-slice_fusion.3
  911.4 2.3 convolution_dynamic-update-slice_fusion.6
  918.1 2.3 convolution_dynamic-update-slice_fusion.5
  920.4 9.2 fusion.165
  929.6 4.8 convolution_add_fusion.1
  934.4 5.9 fusion.37
  940.3 38.8 %all-reduce.4 = (f32[2048]{0:T(1024)S(1)}, f32[2048]{0:T(1024)S(1)}) all-reduce(f32[2048]{0:T(1024)S(1)} %get-tuple-element.13, f32[2048]{0:T(1024)S(1)} %copy-done.53), channel_id=2, replica_groups=mesh['wide'=8,'narrow'=4] {'wide','narrow'}, use_global_device_ids=true, to_apply=%region_17.18.clone | all-reduce | flops 4096 | bytes 32768
  980.3 5.1 fusion.36
  985.4 19.3 fusion.31
  1004.7 1354.7 %reduce-scatter.2.cloned.1.call-done = f32[64,21504]{1,0:T(8,128)} async-done(((f32[2048,21504]{1,0:T(8,128)}), f32[64,21504]{1,0:T(8,128)}) %reduce-scatter.2.cloned.1.call-update) | async-done | bytes 5505040 | tf_op jit(solution)/shard_map/reduce_scatter | solution.py:335
  2359.4 1.5 fusion.153
  2360.9 2.3 fusion.152
  2363.2 4.4 fusion.151
  (190 shorter events, 30.3 us)
Async XLA Ops:
  7.2 7.8 copy-start.8
  7.2 8.2 copy-start.54
  7.2 8.4 copy-start.55
  7.2 63.6 %all-gather.9.cloned.1.call-start = ((), (), s32[]{:S(2)}) async-start(), calls=%async_computation.1 | async-start | bytes 2162688 | tf_op jit(solution)/shard_map/all_gather | solution.py:54
  8.8 141.2 %all-gather.11.cloned.1.call-start = ((), (), s32[]{:S(2)}) async-start(), calls=%async_computation.2 | async-start | bytes 8650752 | tf_op jit(solution)/shard_map/all_gather | solution.py:52
  9.5 219.4 %all-gather.13.cloned.1.call-start = ((), (), s32[]{:S(2)}) async-start(), calls=%async_computation.3 | async-start | bytes 8650752 | tf_op jit(solution)/shard_map/all_gather | solution.py:247
  10.3 364.6 %all-gather.17.cloned.1.call-start = ((), (), s32[]{:S(2)}) async-start(), calls=%async_computation.5 | async-start | bytes 23789568 | tf_op jit(solution)/shard_map/all_gather | solution.py:71
  10.8 509.5 %all-gather.15.cloned.1.call-start = ((), (), s32[]{:S(2)}) async-start(), calls=%async_computation.4 | async-start | bytes 23789568 | tf_op jit(solution)/shard_map/all_gather | solution.py:70
  11.4 654.4 %all-gather.19.cloned.1.call-start = ((), (), s32[]{:S(2)}) async-start(), calls=%async_computation.6 | async-start | bytes 23789568 | tf_op jit(solution)/shard_map/all_gather | solution.py:257
  12.0 917.6 %all-gather.21.cloned.1.call-start = ((), (), s32[]{:S(2)}) async-start(), calls=%async_computation.7 | async-start | bytes 1081344 | tf_op jit(solution)/shard_map/all_gather | solution.py:320
  12.8 921.7 %all-gather.23.cloned.1.call-start = ((), (), s32[]{:S(2)}) async-start(), calls=%async_computation.8 | async-start | bytes 1081344 | tf_op jit(solution)/shard_map/all_gather | solution.py:321
  13.5 2345.9 %reduce-scatter.2.cloned.1.call-start = ((), (), s32[]{:S(2)}) async-start(), calls=%async_computation.9 | async-start | bytes 181665792 | tf_op jit(solution)/shard_map/reduce_scatter | solution.py:335
  14.3 807.3 %copy-start.44 = (f32[320]{0:T(512)}, f32[320]{0:T(512)S(1)}, u32[]{:S(2)}) copy-start(f32[320]{0:T(512)S(1)} %fusion.123) | copy-start | bytes 3844
  15.3 134.6 %copy-start.46 = (f32[320]{0:T(512)}, f32[320]{0:T(512)S(1)}, u32[]{:S(2)}) copy-start(f32[320]{0:T(512)S(1)} %add_rsqrt_fusion.1) | copy-start | bytes 3844
  58.0 92.0 %copy-start.41 = (f32[2048]{0:T(1024)}, f32[2048]{0:T(1024)S(1)}, u32[]{:S(2)}) copy-start(f32[2048]{0:T(1024)S(1)} %convert_element_type.106) | copy-start | bytes 24580
  58.2 5.6 copy-start.21
  58.3 105.1 %copy-start.23 = (f32[320,64]{0,1:T(8,128)}, f32[320,64]{0,1:T(8,128)S(1)}, u32[]{:S(2)}) copy-start(f32[320,64]{0,1:T(8,128)S(1)} %pad_maximum_fusion.9) | copy-start | bytes 245764
  73.0 110.3 %copy-start.28 = (bf16[320,256]{1,0:T(8,128)(2,1)}, bf16[320,256]{1,0:T(8,128)(2,1)S(1)}, u32[]{:S(2)}) copy-start(bf16[320,256]{1,0:T(8,128)(2,1)S(1)} %add_convert_fusion.1) | copy-start | bytes 491524
  173.5 3.3 copy-start.25
  173.7 1.5 copy-start.33
  174.6 2.2 copy-start
  175.2 565.0 %copy-start.49 = (f32[8,320]{1,0:T(8,128)}, f32[8,320]{1,0:T(8,128)S(1)}, u32[]{:S(2)}) copy-start(f32[8,320]{1,0:T(8,128)S(1)} %log_add_fusion.2) | copy-start | bytes 30724
  177.6 2.2 copy-start.2
  178.2 583.2 %copy-start.51 = (f32[8,320]{1,0:T(8,128)}, f32[8,320]{1,0:T(8,128)S(1)}, u32[]{:S(2)}) copy-start(f32[8,320]{1,0:T(8,128)S(1)} %log_add_fusion.1) | copy-start | bytes 30724
  180.0 1.5 copy-start.26
  180.9 2.2 copy-start.4
  183.3 1.4 copy-start.27
  184.1 2.0 copy-start.6
  186.1 42.8 %copy-start.38 = (bf16[64,8,320]{2,0,1:T(8,128)(2,1)S(1)}, bf16[64,8,320]{2,0,1:T(8,128)(2,1)}, u32[]{:S(2)}) copy-start(bf16[64,8,320]{2,0,1:T(8,128)(2,1)} %fusion.80) | copy-start | bytes 983044
  186.1 42.8 %copy-start.39 = (bf16[64,8,320]{2,0,1:T(8,128)(2,1)S(1)}, bf16[64,8,320]{2,0,1:T(8,128)(2,1)}, u32[]{:S(2)}) copy-start(bf16[64,8,320]{2,0,1:T(8,128)(2,1)} %fusion.79) | copy-start | bytes 983044
  186.1 42.8 %copy-start.40 = (bf16[64,8,320]{2,0,1:T(8,128)(2,1)S(1)}, bf16[64,8,320]{2,0,1:T(8,128)(2,1)}, u32[]{:S(2)}) copy-start(bf16[64,8,320]{2,0,1:T(8,128)(2,1)} %fusion.78) | copy-start | bytes 983044
  236.2 1.5 copy-start.13
  238.0 282.3 %copy-start.10 = (bf16[320,2048]{1,0:T(8,128)(2,1)}, bf16[320,2048]{1,0:T(8,128)(2,1)S(1)}, u32[]{:S(2)}) copy-start(bf16[320,2048]{1,0:T(8,128)(2,1)S(1)} %multiply_convert_fusion.3) | copy-start | bytes 3932164
  389.8 276.1 %copy-start.15 = (bf16[320,2048]{1,0:T(8,128)(2,1)S(1)}, bf16[320,2048]{1,0:T(8,128)(2,1)}, u32[]{:S(2)}) copy-start(bf16[320,2048]{1,0:T(8,128)(2,1)} %param.14) | copy-start | bytes 3932164
  686.3 14.3 copy-start.14
  805.2 9.4 copy-start.24
  844.8 23.0 copy-start.11
  888.6 10.0 copy-start.17
  888.6 10.0 copy-start.18
  898.6 1.9 copy-start.12
  898.6 1.9 copy-start.22
  900.5 1.3 copy-start.9
  900.5 1.3 copy-start.42
  900.5 1.3 copy-start.47
  901.8 8.7 copy-start.16
  901.8 8.7 copy-start.31
  901.8 8.7 copy-start.32
  901.8 8.8 copy-start.34
  901.8 8.8 copy-start.35
  901.8 8.8 copy-start.36
  901.8 8.8 copy-start.37
  910.5 3.2 copy-start.7
  910.5 3.2 copy-start.20
  911.4 3.6 copy-start.5
  911.4 3.6 copy-start.19
  913.7 2.5 copy-start.3
  913.7 2.5 copy-start.52
  915.0 2.4 copy-start.1
  915.0 2.4 copy-start.50
  920.4 9.2 copy-start.30
  929.6 4.8 copy-start.43
  929.6 4.8 copy-start.48
  934.4 5.9 copy-start.53
  980.3 5.1 copy-start.45
  (1 other events, 0.7 us)
Sparse Core Ops, SparseCore 0:
  11.5 59.1 all-gather.8
  73.7 76.2 all-gather.10
  152.9 75.9 all-gather.12
  231.6 143.1 all-gather.16
  377.5 142.7 all-gather.14
  523.0 142.7 all-gather.18
  668.8 51.9 all-gather.20
  723.8 52.6 all-gather.22
  920.5 1438.8 reduce-scatter.1
